TPU v7x, 32 devices: a whole 2x2x4 slice. The times are simulated.
32 devices in a mesh: grp: 2 (over x), wide: 16 (over z, y, core).
Axes of the slice: x: 2, y: 2, z: 4, core: 2. Of those that a mesh axis runs over, the one named last changes fastest.
Arguments:
- hidden_in: bfloat16 [128, 4096], P(('grp', 'wide')), parts along dimension 0, may hold values from -6 to 6
- ffn_gain: float32 [4096], replicated, may hold values from 0.1 to 1.9
- gate_weight: bfloat16 [4096, 14336], P(None, 'wide'), may hold values from -0.09375 to 0.09375
- up_weight: bfloat16 [4096, 14336], P(None, 'wide'), may hold values from -0.09375 to 0.09375
- down_weight: bfloat16 [14336, 4096], P('wide'), may hold values from -0.046875 to 0.046875
- final_gain: float32 [4096], replicated, may hold values from 0.1 to 1.9
- codes: bfloat16 [256, 128, 4096], P(('grp', 'wide')), parts along dimension 0, may hold values from -1 to 1
- scales: float32 [256, 128, 32], P(('grp', 'wide')), parts along dimension 0, may hold values from 0.5 to 5
- counts: int32 [256], P('grp'), parts along dimension 0, may hold values from 1 to 128, 10240 in all
- list_slot: int32 [256], P('grp'), parts along dimension 0, may hold values from 0 to 127, as said below
- probes: int32 [128, 8], P(('grp', 'wide')), parts along dimension 0, may hold values from 0 to 127, as said below
Outputs:
- top_scores: float32 [128, 8], P(('grp', 'wide')), parts along dimension 0
There are 2 independent parts, one for each index of `grp`. A program takes and returns all parts, laid end to end along the dimension named above; an argument that names none is the same for every part. Nothing has to cross between parts.
Inputs may be any that keep to these rules, and one draw needn't show every extreme that they name: Each query names 8 different lists. List l is held by device list_slot[l] // 8; of the 32 probes of one device's queries at most 2 name lists held by one device, and some devices are named 2 times by the queries of every device. `list_slot`: each storage row holds exactly one list. The valid rows of a list are its first counts[l] rows; some list is full.
All inputs are finite; a program needn't handle non-finite values.
Results may differ from a plain program's by a relative error of at most 0.002.
Values may be sent and summed in bfloat16 or wider, within the bound.
No kernel may reach another device: no remote copies, remote signals or barrier semaphores. Data moves between devices by JAX's collectives and lax.ppermute only.
A program may use at most 128 MiB of HBM per device.

v0:
```python
import jax
import jax.numpy as jnp
from jax import lax
from jax.sharding import PartitionSpec as P

PROBES = 8
K_TOP = 8
floor_score = -1e30


def best_values(values, count):
    return -jnp.sort(-values, axis=-1)[..., :count]


def lookup_pairs(probe_ids, list_slot, counts, lists_dev):
    flat_ids = probe_ids.reshape(-1)
    listing = jnp.arange(list_slot.shape[0], dtype=jnp.int32)
    matches = flat_ids[:, None] == listing[None, :]
    slot_of = jnp.sum(jnp.where(matches, list_slot[None, :], 0), axis=1)
    rows_of = jnp.sum(jnp.where(matches, counts[None, :], 0), axis=1)
    return (slot_of // lists_dev, slot_of % lists_dev, rows_of)


def copy_rank(owner):
    pair_total = owner.shape[-1]
    same_owner = owner[..., :, None] == owner[..., None, :]
    position = jnp.arange(pair_total, dtype=jnp.int32)
    earlier = position[:, None] > position[None, :]
    return jnp.sum(same_owner & earlier, axis=-1)


def embed(total, final_gain):
    scaled = final_gain * total
    return (scaled * lax.rsqrt(jnp.sum(scaled * scaled, axis=-1, keepdims=True) + 1e-06)).astype(
        jnp.bfloat16
    )


def score_lists(received, codes, scales):
    pair_rows, width = received.shape
    blocks = width // 128
    stored = codes.shape[0] * codes.shape[1]
    partial_sums = jnp.einsum(
        "mbk,rbk->bmr",
        received.reshape(pair_rows, blocks, 128),
        codes.reshape(stored, blocks, 128),
        preferred_element_type=jnp.float32,
    )
    return jnp.einsum(
        "bmr,rb->mr", partial_sums, scales.reshape(stored, blocks), precision=lax.Precision.HIGHEST
    )


def answer(recv_queries, recv_meta, codes, scales):
    sources, slots, width = recv_queries.shape
    lists_dev, list_rows = (codes.shape[0], codes.shape[1])
    table = score_lists(recv_queries.reshape(sources * slots, width), codes, scales)
    table = table.reshape(sources * slots, lists_dev, list_rows)
    local = recv_meta[..., 0].reshape(-1)
    valid_rows = recv_meta[..., 1].reshape(-1)
    pick_mask = local[:, None] == jnp.arange(lists_dev, dtype=jnp.int32)[None, :]
    picked = jnp.sum(jnp.where(pick_mask[:, :, None], table, 0.0), axis=1)
    alive = jnp.arange(list_rows, dtype=jnp.int32)[None, :] < valid_rows[:, None]
    masked = jnp.where(alive, picked, floor_score)
    kept = masked.reshape(sources, slots, list_rows)
    return lax.all_to_all(kept, "wide", split_axis=0, concat_axis=0, tiled=True)


def body(
    hidden_in,
    ffn_gain,
    gate_weight,
    up_weight,
    down_weight,
    final_gain,
    codes,
    scales,
    counts,
    list_slot,
    probes,
):
    q_dev, width = hidden_in.shape
    wide_count = lax.axis_size("wide")
    lists_dev = codes.shape[0]
    pair_total = q_dev * PROBES
    capacity = (pair_total + wide_count - 1) // wide_count
    own_rows = hidden_in.astype(jnp.float32)
    rows = lax.all_gather(hidden_in, "wide", axis=0, tiled=True).astype(jnp.float32)
    normed = (
        rows * lax.rsqrt(jnp.mean(rows * rows, axis=-1, keepdims=True) + 1e-05) * ffn_gain
    ).astype(jnp.bfloat16)
    gate = jnp.dot(normed, gate_weight, preferred_element_type=jnp.float32)
    upward = jnp.dot(normed, up_weight, preferred_element_type=jnp.float32)
    activated = (jax.nn.silu(gate) * upward).astype(jnp.bfloat16)
    owner, local, valid_rows = lookup_pairs(probes, list_slot, counts, lists_dev)
    target = owner * capacity + copy_rank(owner)
    mine = lax.psum_scatter(
        jnp.dot(activated, down_weight, preferred_element_type=jnp.float32),
        "wide",
        scatter_dimension=0,
        tiled=True,
    )
    embedded = embed(own_rows + mine, final_gain)
    slot_ids = jnp.arange(wide_count * capacity, dtype=jnp.int32)
    placing = slot_ids[:, None] == target[None, :]
    pair_vectors = jnp.repeat(embedded, PROBES, axis=0)
    send_queries = jnp.dot(
        placing.astype(jnp.bfloat16), pair_vectors, preferred_element_type=jnp.float32
    ).astype(jnp.bfloat16)
    send_queries = send_queries.reshape(wide_count, capacity, width)
    pair_meta = jnp.stack([local, valid_rows], axis=1)
    send_meta = jnp.sum(jnp.where(placing[:, :, None], pair_meta[None, :, :], 0), axis=1).reshape(
        wide_count, capacity, 2
    )
    returned = answer(
        lax.all_to_all(send_queries, "wide", split_axis=0, concat_axis=0, tiled=True),
        lax.all_to_all(send_meta, "wide", split_axis=0, concat_axis=0, tiled=True),
        codes,
        scales,
    )
    flat_back = returned.reshape(wide_count * capacity, returned.shape[-1])
    per_pair = jnp.take(flat_back, target, axis=0).reshape(q_dev, -1)
    return best_values(per_pair, K_TOP)


def solution(mesh):
    in_specs = (
        P(("grp", "wide"), None),
        P(),
        P(None, "wide"),
        P(None, "wide"),
        P("wide", None),
        P(),
        P(("grp", "wide"), None, None),
        P(("grp", "wide"), None, None),
        P("grp"),
        P("grp"),
        P(("grp", "wide"), None),
    )
    out_specs = P(("grp", "wide"), None)
    return jax.shard_map(body, mesh=mesh, in_specs=in_specs, out_specs=out_specs, check_vma=False)
```

profile of v0, /device:TPU:0, one launch (start us, length us, event | category | flops | bytes accessed | tf_op | source)
XLA Modules:
  0.0 191.7 jit_solution(12854098284234946222)
XLA Ops:
  6.5 24.9 %all-gather = bf16[16,4,4096]{2,1,0:T(4,128)(2,1)S(1)} all-gather(bf16[1,4,4096]{2,1,0:T(4,128)(2,1)} %bitcast.60), channel_id=1, replica_groups=mesh['grp'=2,'wide'=16] {'wide'}, dimensions={0}, use_global_device_ids=true | all-gather | bytes 557056 | tf_op jit(solution)/shard_map/all_gather | solution.py:88
  31.6 0.2 multiply_reduce_fusion.1
  31.7 4.5 %fusion.24 = f32[64,896]{1,0:T(8,128)S(1)} fusion(bf16[4096,896]{1,0:T(8,128)(2,1)} %param.13, f32[64,4096]{1,0:T(8,128)S(1)} %reshape.240, f32[4096]{0:T(1024)} %param.12, f32[64]{0:T(128)S(1)} %add_rsqrt_fusion.1), kind=kOutput, calls=%fused_computation.69 | convolution fusion | flops 470548480 | bytes 8634624 | tf_op jit(solution)/shard_map/dot_general | solution.py:92
  36.3 9.0 %fusion.5 = f32[64,4096]{1,0:T(8,128)} fusion(bf16[896,4096]{1,0:T(8,128)(2,1)} %param.15, bf16[4096,896]{1,0:T(8,128)(2,1)} %param.14, f32[64,896]{1,0:T(8,128)S(1)} %fusion.24, f32[64,4096]{1,0:T(8,128)S(1)} %reshape.240, f32[4096]{0:T(1024)S(1)} %copy-done.3, f32[64]{0:T(128)S(1)} %add_rsqrt_fusion.1), kind=kOutput, calls=%fused_computation.9 | convolution fusion | flops 940654592 | bytes 17023232 | tf_op jit(solution)/shard_map/dot_general | solution.py:98
  45.4 0.1 eq.74
  45.5 0.2 select_reduce_fusion.1
  45.7 0.2 convert_reduce_fusion
  45.9 0.1 select_reduce_fusion
  46.1 0.1 reshape.223
  46.1 0.6 copy.32
  46.8 3.5 %all-to-all-start = ((s32[16,2,2]{1,2,0:T(2,128)}), s32[16,2,2]{1,2,0:T(2,128)S(1)}, u32[]{:S(2)}, u32[]{:S(2)}) async-start(s32[16,2,2]{1,2,0:T(2,128)} %copy.32), calls=%async_computation | async-start | bytes 32768 | tf_op jit(solution)/shard_map/all_to_all | solution.py:117
  50.3 0.1 reduce_sum.76
  50.4 0.1 reduce_sum.74
  50.4 0.6 dynamic-slice
  51.7 85.2 %all-reduce.3.cloned.1.call-done = f32[64,4096]{1,0:T(8,128)} async-done(((f32[64,4096]{1,0:T(8,128)}), f32[64,4096]{1,0:T(8,128)}) %all-reduce.3.cloned.1.call-update) | async-done | bytes 1048592
  137.0 1.1 multiply_reduce_fusion.2
  138.0 1.0 multiply_convert_fusion.1
  139.0 0.2 convolution_convert_fusion
  139.2 0.9 reshape.225
  140.1 3.8 %all-to-all-start.1 = ((bf16[16,2,4096]{2,1,0:T(2,128)(2,1)}), bf16[16,2,4096]{2,1,0:T(2,128)(2,1)S(1)}, u32[]{:S(2)}, u32[]{:S(2)}) async-start(bf16[16,2,4096]{2,1,0:T(2,128)(2,1)} %reshape.225), calls=%async_computation.1 | async-start | bytes 524288 | tf_op jit(solution)/shard_map/all_to_all | solution.py:116
  144.0 9.4 %copy.47 = bf16[128,8,32,128]{3,2,1,0:T(8,128)(2,1)} copy(bf16[128,8,32,128]{3,1,2,0:T(8,128)(2,1)} %bitcast.57) | data formatting | bytes 16777216
  153.5 0.1 eq.84
  153.6 0.3 all-to-all-done.1
  153.9 0.2 reshape_reshape.3
  154.2 12.5 %multiply_reduce_fusion = f32[1024,32]{0,1:T(8,128)S(1)} fusion(bf16[1024,32,128]{2,1,0:T(8,128)(2,1)} %bitcast.58, f32[1024,32]{0,1:T(8,128)S(1)} %copy_bitcast_fusion, bf16[32,32,128]{2,1,0:T(8,128)(2,1)S(1)} %reshape_reshape.3), kind=kOutput, calls=%fused_computation.4 | convolution fusion | flops 270499840 | bytes 8912896 | tf_op jit(solution)/shard_map/mbk,rbk->bmr/dot_general | solution.py:43
  166.7 0.1 fusion.13
  166.9 0.7 compare_select_fusion
  167.5 5.7 %all-to-all-start.2 = ((f32[16,2,128]{2,1,0:T(2,128)}), f32[16,2,128]{2,1,0:T(2,128)S(1)}, u32[]{:S(2)}, u32[]{:S(2)}) async-start(f32[16,2,128]{2,1,0:T(2,128)} %compare_select_fusion), calls=%async_computation.2 | async-start | bytes 32768 | tf_op jit(solution)/shard_map/all_to_all | solution.py:66
  173.3 6.5 %all-to-all-done.2 = f32[16,2,128]{2,1,0:T(2,128)S(1)} async-done(((f32[16,2,128]{2,1,0:T(2,128)}), f32[16,2,128]{2,1,0:T(2,128)S(1)}, u32[]{:S(2)}, u32[]{:S(2)}) %all-to-all-start.2) | async-done | bytes 16416 | tf_op jit(solution)/shard_map/all_to_all | solution.py:66
  179.8 0.6 gather_fusion
  180.4 3.9 %sort_prefixfusion = f32[4,8]{1,0:T(4,128)S(1)} fusion(f32[4,1024]{1,0:T(4,128)S(1)} %select_negate_fusion), kind=kCustom, calls=%sort.15.sort_prefix | custom fusion | flops 49152 | bytes 16512 | tf_op jit(solution)/shard_map/jit(sort)/sort | solution.py:12
  184.3 0.6 neg.12
  (36 shorter events, 0.5 us)
Async XLA Ops:
  6.5 45.2 %copy-start = (f32[8,128,32]{1,2,0:T(8,128)S(1)}, f32[8,128,32]{1,2,0:T(8,128)}, u32[]{:S(2)}) copy-start(f32[8,128,32]{1,2,0:T(8,128)} %param.18) | copy-start | bytes 393220
  6.5 29.7 %copy-start.3 = (f32[4096]{0:T(1024)S(1)}, f32[4096]{0:T(1024)}, u32[]{:S(2)}) copy-start(f32[4096]{0:T(1024)} %param.12) | copy-start | bytes 49156
  6.5 130.4 %all-reduce.3.cloned.1.call-start = ((), (), s32[]{:S(2)}) async-start(), calls=%async_computation.3 | async-start | bytes 2097152
  36.3 9.1 %copy-start.4 = (s32[4,8]{1,0:T(4,128)S(1)}, s32[4,8]{1,0:T(4,128)}, u32[]{:S(2)}) copy-start(s32[4,8]{1,0:T(4,128)} %param.21) | copy-start | bytes 388
  36.3 9.2 %copy-start.5 = (s32[128]{0:T(128)S(1)}, s32[128]{0:T(128)}, u32[]{:S(2)}) copy-start(s32[128]{0:T(128)} %param.19) | copy-start | bytes 1540
  36.3 9.2 %copy-start.6 = (s32[128]{0:T(128)S(1)}, s32[128]{0:T(128)}, u32[]{:S(2)}) copy-start(s32[128]{0:T(128)} %param.20) | copy-start | bytes 1540
  36.3 14.1 %copy-start.7 = (u32[32]{0:T(128)S(1)}, u32[32]{0:T(128)}, u32[]{:S(2)}) copy-start(u32[32]{0:T(128)} %constant.80) | copy-start | bytes 388
  36.3 100.6 %copy-start.1 = (bf16[4,4096]{1,0:T(4,128)(2,1)S(1)}, bf16[4,4096]{1,0:T(4,128)(2,1)}, u32[]{:S(2)}) copy-start(bf16[4,4096]{1,0:T(4,128)(2,1)} %param.11) | copy-start | bytes 98308
  36.3 100.6 %copy-start.2 = (f32[4096]{0:T(1024)S(1)}, f32[4096]{0:T(1024)}, u32[]{:S(2)}) copy-start(f32[4096]{0:T(1024)} %param.16) | copy-start | bytes 49156
  46.8 93.4 %all-to-all-start = ((s32[16,2,2]{1,2,0:T(2,128)}), s32[16,2,2]{1,2,0:T(2,128)S(1)}, u32[]{:S(2)}, u32[]{:S(2)}) async-start(s32[16,2,2]{1,2,0:T(2,128)} %copy.32), calls=%async_computation | async-start | bytes 32768 | tf_op jit(solution)/shard_map/all_to_all | solution.py:117
  140.1 13.8 %all-to-all-start.1 = ((bf16[16,2,4096]{2,1,0:T(2,128)(2,1)}), bf16[16,2,4096]{2,1,0:T(2,128)(2,1)S(1)}, u32[]{:S(2)}, u32[]{:S(2)}) async-start(bf16[16,2,4096]{2,1,0:T(2,128)(2,1)} %reshape.225), calls=%async_computation.1 | async-start | bytes 524288 | tf_op jit(solution)/shard_map/all_to_all | solution.py:116
  167.5 12.2 %all-to-all-start.2 = ((f32[16,2,128]{2,1,0:T(2,128)}), f32[16,2,128]{2,1,0:T(2,128)S(1)}, u32[]{:S(2)}, u32[]{:S(2)}) async-start(f32[16,2,128]{2,1,0:T(2,128)} %compare_select_fusion), calls=%async_computation.2 | async-start | bytes 32768 | tf_op jit(solution)/shard_map/all_to_all | solution.py:66
Sparse Core Ops, SparseCore 0:
  45.5 91.3 all-reduce.2
where the time goes:
time: 192 us
  waiting for transfers between devices  92 us (48%)
  matrix products  26.3 us (14%)
  blocking collectives  24.9 us (13%)
  between operations  14.3 us (7%)
  local copies, waits for them, and re-layouts  13 us (7%)
  starting transfers between devices  13 us (7%)
  other arithmetic  8.15 us (4%)
    unnamed x2, waiting for transfers between devices  85.2 us
    all_gather x1, blocking collectives, body(): lax.all_gather(hidden_in, 'wide', axis=0, tiled=True).astype(jnp.float32)  24.9 us
    dot_general x1, matrix products, score_lists(): jnp.einsum('mbk,rbk->bmr', received.reshape(pair_rows, blocks, 128), code...  12.5 us
    unnamed x20, local copies, waits for them, and re-layouts  10.2 us
    dot_general x1, matrix products, body(): jnp.dot(activated, down_weight, preferred_element_type=jnp.float32)  9.03 us
    all_to_all x1, waiting for transfers between devices, answer(): return lax.all_to_all(kept, 'wide', split_axis=0, concat_axis=0, tiled=True)  6.49 us
    all_to_all x1, starting transfers between devices, answer(): return lax.all_to_all(kept, 'wide', split_axis=0, concat_axis=0, tiled=True)  5.72 us
    dot_general x1, matrix products, body(): gate = jnp.dot(normed, gate_weight, preferred_element_type=jnp.float32)  4.51 us
  transfers between devices with their start and end apart: 4, of which 3 were waited for; matrix products, arithmetic and copies ran while one was open for 8% of the time, Pallas kernels for 0%

commit v1 on v0

--- a/solution.py
+++ b/solution.py
@@ -6,6 +6,28 @@
 PROBES = 8
 K_TOP = 8
 floor_score = -1e30
+
+
+def in_order(blocks, dim):
+    blocks = jnp.moveaxis(blocks, 0, dim)
+    shape = blocks.shape
+    return blocks.reshape(*shape[:dim], shape[dim] * shape[dim + 1], *shape[dim + 2 :])
+
+
+def doubled(value, axis):
+    length = lax.axis_size(axis)
+    blocks = value[None]
+    for level in range(length.bit_length() - 1):
+        bit = 1 << level
+        received = lax.ppermute(blocks, axis, [(i, i ^ bit) for i in range(length)])
+        both = jnp.stack([blocks, received])
+        upper = lax.axis_index(axis) >> level & 1
+        blocks = jnp.where(upper == 0, both, both[::-1]).reshape(-1, *value.shape)
+    return blocks
+
+
+def doubled_up(array, axis, dim):
+    return in_order(doubled(array, axis), dim)
 
 
 def best_values(values, count):
@@ -85,7 +107,7 @@
     pair_total = q_dev * PROBES
     capacity = (pair_total + wide_count - 1) // wide_count
     own_rows = hidden_in.astype(jnp.float32)
-    rows = lax.all_gather(hidden_in, "wide", axis=0, tiled=True).astype(jnp.float32)
+    rows = doubled_up(hidden_in, "wide", 0).astype(jnp.float32)
     normed = (
         rows * lax.rsqrt(jnp.mean(rows * rows, axis=-1, keepdims=True) + 1e-05) * ffn_gain
     ).astype(jnp.bfloat16)

time: 192 us -> 200 us (1.042)
  blocking collectives: 24.9 us -> 0 us
  waiting for transfers between devices: 92 us -> 111 us
  starting transfers between devices: 13 us -> 22.6 us
  other arithmetic: 8.15 us -> 11 us
    all_gather x1 -> x0, blocking collectives: 24.9 us -> none  [body(): lax.all_gather(hidden_in, 'wide', axis=0, tiled=True).astype(jnp.float32)]
    ppermute x0 -> x4, waiting for transfers between devices: none -> 17.4 us  [doubled(): received = lax.ppermute(blocks, axis, [(i, i ^ bit) for i in range(length)])]
    ppermute x0 -> x4, starting transfers between devices: none -> 7.56 us  [doubled(): received = lax.ppermute(blocks, axis, [(i, i ^ bit) for i in range(length)])]
    unnamed x20 -> x14, local copies, waits for them, and re-layouts: 10.2 us -> 10.2 us
  transfers between devices with their start and end apart: 4 -> 8, of which waited for: 3 -> 6; matrix products, arithmetic and copies ran while one was open for 8% -> 8% of each run, Pallas kernels for 0% -> 0%
where the time goes in v1:
time: 200 us; the launch traced here: 199 us
  waiting for transfers between devices  111 us (56%)
  matrix products  26.3 us (13%)
  starting transfers between devices  22.6 us (11%)
  between operations  14.3 us (7%)
  local copies, waits for them, and re-layouts  14 us (7%)
  other arithmetic  11 us (6%)
    unnamed x2, waiting for transfers between devices  87 us
    ppermute x4, waiting for transfers between devices, doubled(): received = lax.ppermute(blocks, axis, [(i, i ^ bit) for i in range(length)])  17.4 us
    dot_general x1, matrix products, score_lists(): jnp.einsum('mbk,rbk->bmr', received.reshape(pair_rows, blocks, 128), code...  12.5 us
    unnamed x14, local copies, waits for them, and re-layouts  10.2 us
    dot_general x1, matrix products, body(): jnp.dot(activated, down_weight, preferred_element_type=jnp.float32)  9.02 us
    ppermute x4, starting transfers between devices, doubled(): received = lax.ppermute(blocks, axis, [(i, i ^ bit) for i in range(length)])  7.56 us
    all_to_all x1, waiting for transfers between devices, answer(): return lax.all_to_all(kept, 'wide', split_axis=0, concat_axis=0, tiled=True)  6.49 us
    all_to_all x1, starting transfers between devices, answer(): return lax.all_to_all(kept, 'wide', split_axis=0, concat_axis=0, tiled=True)  5.72 us
  transfers between devices with their start and end apart: 8, of which 6 were waited for; matrix products, arithmetic and copies ran while one was open for 8% of the time, Pallas kernels for 0%

profile of v1, /device:TPU:0, one launch (start us, length us, event | category | flops | bytes accessed | tf_op | source)
XLA Modules:
  0.0 199.4 jit_solution(3023043226393728042)
XLA Ops:
  6.5 0.5 collective-permute-start
  7.0 0.8 eq.86
  7.8 0.8 select_reduce_fusion.1
  8.9 0.8 pad_maximum_fusion.3
  9.7 2.6 %collective-permute-start.1 = (bf16[2,4,4096]{2,1,0:T(4,128)(2,1)S(1)}, bf16[2,4,4096]{2,1,0:T(4,128)(2,1)S(1)}, u32[]{:S(2)}, u32[]{:S(2)}) collective-permute-start(bf16[2,4,4096]{2,1,0:T(4,128)(2,1)S(1)} %get-tuple-element.12), channel_id=1, source_target_pairs={{0,2},{1,3},{2,0},{3,1},{4,6},{5,7},{6,4},{7,5},{8,10},{9,11},{10,... | collective-permute-start | bytes 196616 | tf_op jit(solution)/shard_map/ppermute | solution.py:22
  12.4 2.7 %collective-permute-done.1 = bf16[2,4,4096]{2,1,0:T(4,128)(2,1)S(1)} collective-permute-done((bf16[2,4,4096]{2,1,0:T(4,128)(2,1)S(1)}, bf16[2,4,4096]{2,1,0:T(4,128)(2,1)S(1)}, u32[]{:S(2)}, u32[]{:S(2)}) %collective-permute-start.1) | collective-permute-done | bytes 65568 | tf_op jit(solution)/shard_map/ppermute | solution.py:22
  15.2 1.9 collective-permute-start.2
  17.1 3.5 %collective-permute-done.2 = bf16[4,4,4096]{2,1,0:T(4,128)(2,1)S(1)} collective-permute-done((bf16[4,4,4096]{2,1,0:T(4,128)(2,1)S(1)}, bf16[4,4,4096]{2,1,0:T(4,128)(2,1)S(1)}, u32[]{:S(2)}, u32[]{:S(2)}) %collective-permute-start.2) | collective-permute-done | bytes 131104 | tf_op jit(solution)/shard_map/ppermute | solution.py:22
  20.9 2.6 %collective-permute-start.3 = (bf16[8,4,4096]{2,1,0:T(4,128)(2,1)S(1)}, bf16[8,4,4096]{2,1,0:T(4,128)(2,1)S(1)}, u32[]{:S(2)}, u32[]{:S(2)}) collective-permute-start(bf16[8,4,4096]{2,1,0:T(4,128)(2,1)S(1)} %bitcast.73), channel_id=1, source_target_pairs={{0,8},{1,9},{2,10},{3,11},{4,12},{5,13},{6,14},{7,15},{8,0},{9,1},... | collective-permute-start | bytes 786440 | tf_op jit(solution)/shard_map/ppermute | solution.py:22
  23.5 11.2 %collective-permute-done.3 = bf16[8,4,4096]{2,1,0:T(4,128)(2,1)S(1)} collective-permute-done((bf16[8,4,4096]{2,1,0:T(4,128)(2,1)S(1)}, bf16[8,4,4096]{2,1,0:T(4,128)(2,1)S(1)}, u32[]{:S(2)}, u32[]{:S(2)}) %collective-permute-start.3) | collective-permute-done | bytes 262176 | tf_op jit(solution)/shard_map/ppermute | solution.py:22
  34.7 0.4 pad_maximum_fusion
  35.3 0.5 multiply_reduce_fusion.1
  35.8 0.4 reshape.253
  36.3 4.5 %fusion.27 = f32[64,896]{1,0:T(8,128)S(1)} fusion(bf16[4096,896]{1,0:T(8,128)(2,1)} %param.13, f32[64,4096]{1,0:T(8,128)S(1)} %reshape.253, f32[4096]{0:T(1024)} %param.12, f32[64]{0:T(128)S(1)} %rsqrt.20), kind=kOutput, calls=%fused_computation.80 | convolution fusion | flops 470548480 | bytes 8634624 | tf_op jit(solution)/shard_map/dot_general | solution.py:114
  40.8 9.0 %fusion.5 = f32[64,4096]{1,0:T(8,128)} fusion(bf16[896,4096]{1,0:T(8,128)(2,1)} %param.15, bf16[4096,896]{1,0:T(8,128)(2,1)} %param.14, f32[64,896]{1,0:T(8,128)S(1)} %fusion.27, f32[64,4096]{1,0:T(8,128)S(1)} %reshape.253, f32[4096]{0:T(1024)S(1)} %copy-done.3, f32[64]{0:T(128)S(1)} %rsqrt.20), kind=kOutput, calls=%fused_computation.9 | convolution fusion | flops 940654592 | bytes 17023232 | tf_op jit(solution)/shard_map/dot_general | solution.py:120
  50.1 0.6 copy.32
  50.7 5.5 %all-to-all-start = ((s32[16,2,2]{1,2,0:T(2,128)}), s32[16,2,2]{1,2,0:T(2,128)S(1)}, u32[]{:S(2)}, u32[]{:S(2)}) async-start(s32[16,2,2]{1,2,0:T(2,128)} %copy.32), calls=%async_computation | async-start | bytes 32768 | tf_op jit(solution)/shard_map/all_to_all | solution.py:139
  56.4 0.6 dynamic-slice
  57.6 87.0 %all-reduce.3.cloned.1.call-done = f32[64,4096]{1,0:T(8,128)} async-done(((f32[64,4096]{1,0:T(8,128)}), f32[64,4096]{1,0:T(8,128)}) %all-reduce.3.cloned.1.call-update) | async-done | bytes 1048592
  144.6 1.1 multiply_reduce_fusion.2
  145.7 1.0 multiply_convert_fusion.1
  146.9 0.9 reshape.248
  147.8 3.8 %all-to-all-start.1 = ((bf16[16,2,4096]{2,1,0:T(2,128)(2,1)}), bf16[16,2,4096]{2,1,0:T(2,128)(2,1)S(1)}, u32[]{:S(2)}, u32[]{:S(2)}) async-start(bf16[16,2,4096]{2,1,0:T(2,128)(2,1)} %reshape.248), calls=%async_computation.1 | async-start | bytes 524288 | tf_op jit(solution)/shard_map/all_to_all | solution.py:138
  151.7 9.4 %copy.47 = bf16[128,8,32,128]{3,2,1,0:T(8,128)(2,1)} copy(bf16[128,8,32,128]{3,1,2,0:T(8,128)(2,1)} %bitcast.70) | data formatting | bytes 16777216
  161.3 0.3 all-to-all-done.1
  161.8 12.5 %multiply_reduce_fusion = f32[1024,32]{0,1:T(8,128)S(1)} fusion(bf16[1024,32,128]{2,1,0:T(8,128)(2,1)} %bitcast.71, f32[1024,32]{0,1:T(8,128)S(1)} %copy_bitcast_fusion, bf16[32,32,128]{2,1,0:T(8,128)(2,1)S(1)} %reshape_reshape.4), kind=kOutput, calls=%fused_computation.4 | convolution fusion | flops 270499840 | bytes 8912896 | tf_op jit(solution)/shard_map/mbk,rbk->bmr/dot_general | solution.py:65
  174.6 0.7 compare_select_fusion
  175.2 5.7 %all-to-all-start.2 = ((f32[16,2,128]{2,1,0:T(2,128)}), f32[16,2,128]{2,1,0:T(2,128)S(1)}, u32[]{:S(2)}, u32[]{:S(2)}) async-start(f32[16,2,128]{2,1,0:T(2,128)} %compare_select_fusion), calls=%async_computation.2 | async-start | bytes 32768 | tf_op jit(solution)/shard_map/all_to_all | solution.py:88
  181.0 6.5 %all-to-all-done.2 = f32[16,2,128]{2,1,0:T(2,128)S(1)} async-done(((f32[16,2,128]{2,1,0:T(2,128)}), f32[16,2,128]{2,1,0:T(2,128)S(1)}, u32[]{:S(2)}, u32[]{:S(2)}) %all-to-all-start.2) | async-done | bytes 16416 | tf_op jit(solution)/shard_map/all_to_all | solution.py:88
  187.5 0.6 gather_fusion
  188.1 3.9 %sort_prefixfusion = f32[4,8]{1,0:T(4,128)S(1)} fusion(f32[4,1024]{1,0:T(4,128)S(1)} %select_negate_fusion), kind=kCustom, calls=%sort.15.sort_prefix | custom fusion | flops 49152 | bytes 16512 | tf_op jit(solution)/shard_map/jit(sort)/sort | solution.py:34
  192.0 0.6 neg.12
  (46 shorter events, 2.3 us)
Async XLA Ops:
  6.5 51.1 %copy-start = (f32[8,128,32]{1,2,0:T(8,128)S(1)}, f32[8,128,32]{1,2,0:T(8,128)}, u32[]{:S(2)}) copy-start(f32[8,128,32]{1,2,0:T(8,128)} %param.18) | copy-start | bytes 393220
  6.5 138.1 %all-reduce.3.cloned.1.call-start = ((), (), s32[]{:S(2)}) async-start(), calls=%async_computation.3 | async-start | bytes 2097152
  6.5 2.3 %collective-permute-start = (bf16[1,4,4096]{2,1,0:T(4,128)(2,1)}, bf16[1,4,4096]{2,1,0:T(4,128)(2,1)S(1)}, u32[]{:S(2)}, u32[]{:S(2)}) collective-permute-start(bf16[1,4,4096]{2,1,0:T(4,128)(2,1)} %bitcast.77), channel_id=1, source_target_pairs={{0,1},{1,0},{2,3},{3,2},{4,5},{5,4},{6,7},{7,6},{8,9},{9,8},{10,11... | collective-permute-start | bytes 98312 | tf_op jit(solution)/shard_map/ppermute | solution.py:22
  9.7 5.3 %collective-permute-start.1 = (bf16[2,4,4096]{2,1,0:T(4,128)(2,1)S(1)}, bf16[2,4,4096]{2,1,0:T(4,128)(2,1)S(1)}, u32[]{:S(2)}, u32[]{:S(2)}) collective-permute-start(bf16[2,4,4096]{2,1,0:T(4,128)(2,1)S(1)} %get-tuple-element.12), channel_id=1, source_target_pairs={{0,2},{1,3},{2,0},{3,1},{4,6},{5,7},{6,4},{7,5},{8,10},{9,11},{10,... | collective-permute-start | bytes 196616 | tf_op jit(solution)/shard_map/ppermute | solution.py:22
  15.2 5.4 %collective-permute-start.2 = (bf16[4,4,4096]{2,1,0:T(4,128)(2,1)S(1)}, bf16[4,4,4096]{2,1,0:T(4,128)(2,1)S(1)}, u32[]{:S(2)}, u32[]{:S(2)}) collective-permute-start(bf16[4,4,4096]{2,1,0:T(4,128)(2,1)S(1)} %bitcast.75), channel_id=1, source_target_pairs={{0,4},{1,5},{2,6},{3,7},{4,0},{5,1},{6,2},{7,3},{8,12},{9,13},{10,... | collective-permute-start | bytes 393224 | tf_op jit(solution)/shard_map/ppermute | solution.py:22
  20.8 20.0 %copy-start.3 = (f32[4096]{0:T(1024)S(1)}, f32[4096]{0:T(1024)}, u32[]{:S(2)}) copy-start(f32[4096]{0:T(1024)} %param.12) | copy-start | bytes 49156
  20.9 13.8 %collective-permute-start.3 = (bf16[8,4,4096]{2,1,0:T(4,128)(2,1)S(1)}, bf16[8,4,4096]{2,1,0:T(4,128)(2,1)S(1)}, u32[]{:S(2)}, u32[]{:S(2)}) collective-permute-start(bf16[8,4,4096]{2,1,0:T(4,128)(2,1)S(1)} %bitcast.73), channel_id=1, source_target_pairs={{0,8},{1,9},{2,10},{3,11},{4,12},{5,13},{6,14},{7,15},{8,0},{9,1},... | collective-permute-start | bytes 786440 | tf_op jit(solution)/shard_map/ppermute | solution.py:22
  40.8 15.6 %copy-start.4 = (u32[32]{0:T(128)S(1)}, u32[32]{0:T(128)}, u32[]{:S(2)}) copy-start(u32[32]{0:T(128)} %constant.87) | copy-start | bytes 388
  40.8 103.8 %copy-start.1 = (bf16[4,4096]{1,0:T(4,128)(2,1)S(1)}, bf16[4,4096]{1,0:T(4,128)(2,1)}, u32[]{:S(2)}) copy-start(bf16[4,4096]{1,0:T(4,128)(2,1)} %param.11) | copy-start | bytes 98308
  40.8 103.8 %copy-start.2 = (f32[4096]{0:T(1024)S(1)}, f32[4096]{0:T(1024)}, u32[]{:S(2)}) copy-start(f32[4096]{0:T(1024)} %param.16) | copy-start | bytes 49156
  50.7 97.1 %all-to-all-start = ((s32[16,2,2]{1,2,0:T(2,128)}), s32[16,2,2]{1,2,0:T(2,128)S(1)}, u32[]{:S(2)}, u32[]{:S(2)}) async-start(s32[16,2,2]{1,2,0:T(2,128)} %copy.32), calls=%async_computation | async-start | bytes 32768 | tf_op jit(solution)/shard_map/all_to_all | solution.py:139
  147.8 13.8 %all-to-all-start.1 = ((bf16[16,2,4096]{2,1,0:T(2,128)(2,1)}), bf16[16,2,4096]{2,1,0:T(2,128)(2,1)S(1)}, u32[]{:S(2)}, u32[]{:S(2)}) async-start(bf16[16,2,4096]{2,1,0:T(2,128)(2,1)} %reshape.248), calls=%async_computation.1 | async-start | bytes 524288 | tf_op jit(solution)/shard_map/all_to_all | solution.py:138
  175.2 12.2 %all-to-all-start.2 = ((f32[16,2,128]{2,1,0:T(2,128)}), f32[16,2,128]{2,1,0:T(2,128)S(1)}, u32[]{:S(2)}, u32[]{:S(2)}) async-start(f32[16,2,128]{2,1,0:T(2,128)} %compare_select_fusion), calls=%async_computation.2 | async-start | bytes 32768 | tf_op jit(solution)/shard_map/all_to_all | solution.py:88
Sparse Core Ops, SparseCore 0:
  50.0 94.5 all-reduce.2
